TPU v7x, 32 devices: a whole 2x2x4 slice. The times are simulated.
32 devices in a mesh: groups: 2 (over y), inner: 4 (over z), outer: 4 (over x, core).
Axes of the slice: x: 2, y: 2, z: 4, core: 2. Of those that a mesh axis runs over, the one named last changes fastest.
Arguments:
- queries: bfloat16 [8192, 1024], P(('groups', 'outer', 'inner')), parts along dimension 0, may hold values from -6 to 6
- keys: bfloat16 [8192, 1024], P(('groups', 'outer', 'inner')), parts along dimension 0, may hold values from -6 to 6
- values: bfloat16 [8192, 1024], P(('groups', 'outer', 'inner')), parts along dimension 0, may hold values from -6 to 6
- retain: float32 [8192, 8], P(('groups', 'outer', 'inner')), parts along dimension 0, may hold values from 0.4 to 1
- step: float32 [8192, 8], P(('groups', 'outer', 'inner')), parts along dimension 0, may hold values from 0.000625 to 0.0125
- momentum: float32 [8192, 8], P(('groups', 'outer', 'inner')), parts along dimension 0, may hold values from 0.97 to 0.99
- init_memory: float32 [8, 128, 128], replicated, may hold values from -0.1875 to 0.1875
- init_momentum: float32 [8, 128, 128], replicated, may hold values from -0.1875 to 0.1875
Outputs:
- retrieved: bfloat16 [8192, 1024], P(('groups', 'outer', 'inner')), parts along dimension 0
There are 2 independent parts, one for each index of `groups`. A program takes and returns all parts, laid end to end along the dimension named above; an argument that names none is the same for every part. Nothing has to cross between parts.
All inputs are finite; a program needn't handle non-finite values.
Results may differ from a plain program's by a relative error of at most 0.001.
Values sent between devices are 32-bit elements; how exact they have to be, the bound alone decides.
No kernel may reach another device: no remote copies, remote signals or barrier semaphores. Data moves between devices by JAX's collectives and lax.ppermute only.
A program may use at most 256 MiB of HBM per device.

v0:
```python
import jax
import jax.numpy as jnp
from jax import lax
from jax.sharding import PartitionSpec as P


def carried_in(value, axis, join, neutral):
    count, mine = (lax.axis_size(axis), lax.axis_index(axis))
    pieces = jax.tree.map(lambda part: lax.all_gather(part, axis), value)
    total = jax.tree.map(
        lambda part, zero: jnp.full_like(part, 0) + jnp.asarray(zero, part.dtype), value, neutral
    )

    def turn(position, total):
        longer = join(total, jax.tree.map(lambda part: part[position], pieces))
        return jax.tree.map(lambda new, old: jnp.where(position < mine, new, old), longer, total)

    return lax.fori_loop(0, count - 1, turn, total)


def from_root(block, axis, owner):
    block = jnp.where(lax.axis_index(axis) == owner, block, jnp.zeros_like(block))
    return lax.psum(block, axis)


def unit_rows(source, heads):
    rows = source.astype(jnp.float32).reshape(source.shape[0], heads, -1)
    return rows * lax.rsqrt(jnp.sum(rows * rows, -1, keepdims=True) + 1e-06)


def block_terms(queries, keys, values, retain, step, momentum):
    length = queries.shape[0]
    heads = retain.shape[1]
    precise = lax.Precision.HIGHEST
    query_unit = unit_rows(queries, heads)
    key_unit = unit_rows(keys, heads)
    value_rows = values.astype(jnp.float32).reshape(length, heads, -1)
    key_width = key_unit.shape[2]
    log_retain = jnp.cumsum(jnp.log(retain), 0).T
    log_moment = jnp.cumsum(jnp.log(momentum), 0).T
    position = jnp.arange(length)
    causal = (position[:, None] >= position[None, :])[None]
    retain_decay = jnp.where(
        causal,
        jnp.exp(jnp.where(causal, log_retain[:, :, None] - log_retain[:, None, :], 0.0)),
        0.0,
    )
    momentum_decay = jnp.where(
        causal,
        jnp.exp(jnp.where(causal, log_moment[:, :, None] - log_moment[:, None, :], 0.0)),
        0.0,
    )
    weights = jnp.einsum("htu,hur->htr", retain_decay, momentum_decay, precision=precise)
    carry_scale = jnp.einsum("htu,hu->ht", retain_decay, jnp.exp(log_moment), precision=precise)
    scores = jnp.einsum("thd,rhd->htr", query_unit, key_unit, precision=precise)
    step_rows = step.T
    mixing = scores * weights * step_rows[:, None, :]
    memory_weight = weights[:, -1, :] * step_rows
    moment_weight = jnp.exp(log_moment[:, -1:] - log_moment) * step_rows
    memory_gram = jnp.einsum(
        "rhd,hr,rhe->hde", key_unit, memory_weight, key_unit, precision=precise
    )
    moment_gram = jnp.einsum(
        "rhd,hr,rhe->hde", key_unit, moment_weight, key_unit, precision=precise
    )
    identity = jnp.eye(key_width, dtype=jnp.float32)[None]
    retain_end = jnp.exp(log_retain[:, -1])[:, None, None]
    moment_end = jnp.exp(log_moment[:, -1])[:, None, None]
    carry_end = carry_scale[:, -1][:, None, None]
    upper_rows = jnp.concatenate([retain_end * identity - memory_gram, -moment_gram], axis=2)
    lower_rows = jnp.concatenate([carry_end * identity, moment_end * identity], axis=2)
    transition = jnp.concatenate([upper_rows, lower_rows], axis=1)
    memory_write = jnp.einsum(
        "rhd,hr,rhe->hde", value_rows, memory_weight, key_unit, precision=precise
    )
    moment_write = jnp.einsum(
        "rhd,hr,rhe->hde", value_rows, moment_weight, key_unit, precision=precise
    )
    offset = jnp.concatenate([memory_write, moment_write], axis=2)
    local_terms = (query_unit, key_unit, value_rows, jnp.exp(log_retain), carry_scale, mixing)
    return (transition, offset, local_terms)


def block_output(carried, local_terms):
    query_unit, key_unit, value_rows, retain_scale, carry_scale, mixing = local_terms
    precise = lax.Precision.HIGHEST
    key_width = query_unit.shape[2]
    memory = carried[:, :, :key_width]
    moment_part = carried[:, :, key_width:]
    residual = jnp.einsum("rhd,hed->hre", key_unit, memory, precision=precise) - jnp.transpose(
        value_rows, (1, 0, 2)
    )
    result = retain_scale[:, :, None] * jnp.einsum(
        "thd,hed->hte", query_unit, memory, precision=precise
    )
    result = result + carry_scale[:, :, None] * jnp.einsum(
        "thd,hed->hte", query_unit, moment_part, precision=precise
    )
    result = result - jnp.einsum("htr,hre->hte", mixing, residual, precision=precise)
    return jnp.transpose(result, (1, 0, 2)).reshape(query_unit.shape[0], -1).astype(jnp.bfloat16)


def advance_state(carried, transition, offset):
    return jnp.einsum("hij,hjk->hik", carried, transition, precision=lax.Precision.HIGHEST) + offset


def compose(earlier, later):
    joined = jnp.einsum("hij,hjk->hik", earlier[0], later[0], precision=lax.Precision.HIGHEST)
    return (joined, advance_state(earlier[1], later[0], later[1]))


def apply_earlier(gathered, first_state):
    my_group = lax.axis_index("outer")

    def advance_group(index, carried):
        moved = advance_state(carried, gathered[0][index], gathered[1][index])
        return jnp.where(index < my_group, moved, carried)

    return lax.fori_loop(0, gathered[0].shape[0], advance_group, first_state)


def local(queries, keys, values, retain, step, momentum, init_memory, init_momentum):
    transition, offset, local_terms = block_terms(queries, keys, values, retain, step, momentum)
    identity_maps = (
        jnp.broadcast_to(jnp.eye(transition.shape[1], dtype=jnp.float32), transition.shape),
        jnp.zeros_like(offset),
    )
    before = carried_in((transition, offset), "inner", compose, identity_maps)
    through = compose(before, (transition, offset))
    first_state = jnp.concatenate([init_memory, init_momentum], axis=2)
    last_inner = lax.axis_size("inner") - 1
    group_map = (
        from_root(through[0], "inner", last_inner),
        from_root(through[1], "inner", last_inner),
    )
    gathered = (
        lax.all_gather(group_map[0][None], "outer", axis=0, tiled=True),
        lax.all_gather(group_map[1][None], "outer", axis=0, tiled=True),
    )
    entry_state = apply_earlier(gathered, first_state)
    block_state = advance_state(entry_state, before[0], before[1])
    return block_output(block_state, local_terms)


def solution(mesh):
    placed = (
        P(("groups", "outer", "inner"), None),
        P(("groups", "outer", "inner"), None),
        P(("groups", "outer", "inner"), None),
        P(("groups", "outer", "inner"), None),
        P(("groups", "outer", "inner"), None),
        P(("groups", "outer", "inner"), None),
        P(),
        P(),
    )
    return jax.shard_map(
        local,
        mesh=mesh,
        in_specs=placed,
        out_specs=P(("groups", "outer", "inner"), None),
        check_vma=False,
    )
```

profile of v0, /device:TPU:0, one launch (start us, length us, event | category | flops | bytes accessed | tf_op | source)
XLA Modules:
  0.0 601.0 jit_solution(4477719836671399538)
XLA Ops:
  10.5 2.9 fusion.39
  18.3 2.1 broadcast_multiply_fusion.1
  22.7 2.0 copy.120
  29.2 2.6 copy.125
  32.2 2.3 fusion.44
  38.9 1.8 copy.119
  41.4 74.1 %all-gather.13.cloned.1.call-done = f32[32,128,256]{2,1,0:T(8,128)} async-done(((f32[8,128,256]{2,1,0:T(8,128)}), f32[32,128,256]{2,1,0:T(8,128)}) %all-gather.13.cloned.1.call-update) | async-done | bytes 4194320 | tf_op jit(solution)/shard_map/all_gather | solution.py:9
  115.4 149.8 %all-gather.11.cloned.1.call-done = f32[32,256,256]{2,1,0:T(8,128)} async-done(((f32[8,256,256]{2,1,0:T(8,128)}), f32[32,256,256]{2,1,0:T(8,128)}) %all-gather.11.cloned.1.call-update) | async-done | bytes 8388624 | tf_op jit(solution)/shard_map/all_gather | solution.py:9
  265.4 49.7 %while.30 = (s32[]{:T(128)}, f32[8,256,256]{1,2,0:T(8,128)S(1)}, f32[8,128,256]{1,2,0:T(8,128)}, s32[]{:T(128)}, f32[4,8,256,256]{3,2,1,0:T(8,128)}, /*index=5*/f32[4,8,128,256]{3,2,1,0:T(8,128)}, s32[]{:T(128)}, s32[]{:T(128)}) while((s32[]{:T(128)}, f32[8,256,256]{1,2,0:T(8,128)S(1)}, f32[8,128,256]{1,2,0:T(8,128)}, s32[]{:T(128)}, ...), condition=%wide.region_7.8_spmd.clone, body=%wide.region_6.7_spmd.clone.sunk | while | flops 2417491968 | bytes 25168492 | solution.py:18
  265.4 2.3 constant_dynamic-slice_fusion.5
  270.5 6.1 %fusion.112 = f32[8,128,256]{1,2,0:T(8,128)} fusion(f32[4,8,256,256]{3,2,1,0:T(8,128)} %get-tuple-element.387, s32[]{:T(128)} %get-tuple-element.375, f32[1,8,128,256]{2,3,1,0:T(8,128)S(1)} %copy.193, f32[8,128,256]{1,2,0:T(8,128)S(1)} %copy.218, pred[]{:T(512)S(6)} %compare.3, pred[]{:T(512)S(6)} %lt.44), kind=kOutput, calls=%fused_computation.17.clone.1 | convolution fusion | flops 806354944 | bytes 6293504 | tf_op jit(solution)/shard_map/while/body/eval_jaxpr/hij,hjk->hik/dot_general | solution.py:104
  276.8 5.1 bitcast_select_fusion.2
  281.9 2.3 constant_dynamic-slice_fusion.5
  287.0 6.1 %fusion.112 = f32[8,128,256]{1,2,0:T(8,128)} fusion(f32[4,8,256,256]{3,2,1,0:T(8,128)} %get-tuple-element.387, s32[]{:T(128)} %get-tuple-element.375, f32[1,8,128,256]{2,3,1,0:T(8,128)S(1)} %copy.193, f32[8,128,256]{1,2,0:T(8,128)S(1)} %copy.218, pred[]{:T(512)S(6)} %compare.3, pred[]{:T(512)S(6)} %lt.44), kind=kOutput, calls=%fused_computation.17.clone.1 | convolution fusion | flops 806354944 | bytes 6293504 | tf_op jit(solution)/shard_map/while/body/eval_jaxpr/hij,hjk->hik/dot_general | solution.py:104
  293.3 5.1 bitcast_select_fusion.2
  298.4 2.3 constant_dynamic-slice_fusion.5
  303.5 6.1 %fusion.112 = f32[8,128,256]{1,2,0:T(8,128)} fusion(f32[4,8,256,256]{3,2,1,0:T(8,128)} %get-tuple-element.387, s32[]{:T(128)} %get-tuple-element.375, f32[1,8,128,256]{2,3,1,0:T(8,128)S(1)} %copy.193, f32[8,128,256]{1,2,0:T(8,128)S(1)} %copy.218, pred[]{:T(512)S(6)} %compare.3, pred[]{:T(512)S(6)} %lt.44), kind=kOutput, calls=%fused_computation.17.clone.1 | convolution fusion | flops 806354944 | bytes 6293504 | tf_op jit(solution)/shard_map/while/body/eval_jaxpr/hij,hjk->hik/dot_general | solution.py:104
  309.8 5.1 bitcast_select_fusion.2
  315.1 5.2 fusion.49
  320.3 4.8 select_bitcast_fusion
  325.2 119.8 %all-reduce.3.cloned.1.call-done = (f32[1,8,256,256]{3,2,1,0:T(8,128)}, f32[1,8,128,256]{2,3,1,0:T(8,128)}) async-done(((f32[1,8,256,256]{3,2,1,0:T(8,128)}, f32[1,8,128,256]{2,3,1,0:T(8,128)}), (f32[1,8,256,256]{3,2,1,0:T(8,128)}, f32[1,8,128,256]{2,3,1,0:T(8,128)})) %all-reduce.3.cloned.1.call-update) | async-done | bytes 3145744 | tf_op jit(solution)/shard_map/psum | solution.py:23
  445.0 2.5 copy.133
  452.1 5.1 fusion.66
  458.5 22.6 %all-gather.9.cloned.1.call-done = f32[4,8,128,256]{3,2,1,0:T(8,128)} async-done(((f32[1,8,128,256]{3,2,1,0:T(8,128)}), f32[4,8,128,256]{3,2,1,0:T(8,128)}) %all-gather.9.cloned.1.call-update) | async-done | bytes 4194320 | tf_op jit(solution)/shard_map/all_gather | solution.py:138
  481.2 59.7 %all-gather.7.cloned.1.call-done = f32[4,8,256,256]{3,2,1,0:T(8,128)} async-done(((f32[1,8,256,256]{3,2,1,0:T(8,128)}), f32[4,8,256,256]{3,2,1,0:T(8,128)}) %all-gather.7.cloned.1.call-update) | async-done | bytes 8388624 | tf_op jit(solution)/shard_map/all_gather | solution.py:137
  540.9 41.4 %while.29 = (s32[]{:T(128)}, f32[8,128,256]{1,2,0:T(8,128)}, s32[]{:T(128)}, f32[4,8,256,256]{3,2,1,0:T(8,128)}, f32[4,8,128,256]{3,2,1,0:T(8,128)}, /*index=5*/s32[]{:T(128)}) while((s32[]{:T(128)}, f32[8,128,256]{1,2,0:T(8,128)}, s32[]{:T(128)}, f32[4,8,256,256]{3,2,1,0:T(8,128)}, f32[4,8,128,256]{3,2,1,0:T(8,128)}, ...), condition=%wide.region_11.12_spmd, body=%wide.region_10.11_spmd.sunk | while | flops 805830656 | bytes 16777840 | solution.py:119
  545.3 6.1 %fusion.107 = f32[8,128,256]{1,2,0:T(8,128)} fusion(f32[8,128,256]{1,2,0:T(8,128)S(1)} %copy.216, f32[4,8,256,256]{3,2,1,0:T(8,128)} %get-tuple-element.406, s32[]{:T(128)} %get-tuple-element.397, f32[1,8,128,256]{2,3,1,0:T(8,128)S(1)} %copy-done, pred[]{:T(512)S(6)} %lt.43), kind=kOutput, calls=%fused_computation.5.clone.1 | convolution fusion | flops 805830656 | bytes 6291969 | tf_op jit(solution)/shard_map/while/body/eval_jaxpr/hij,hjk->hik/dot_general | solution.py:104
  555.6 6.1 %fusion.107 = f32[8,128,256]{1,2,0:T(8,128)} fusion(f32[8,128,256]{1,2,0:T(8,128)S(1)} %copy.216, f32[4,8,256,256]{3,2,1,0:T(8,128)} %get-tuple-element.406, s32[]{:T(128)} %get-tuple-element.397, f32[1,8,128,256]{2,3,1,0:T(8,128)S(1)} %copy-done, pred[]{:T(512)S(6)} %lt.43), kind=kOutput, calls=%fused_computation.5.clone.1 | convolution fusion | flops 805830656 | bytes 6291969 | tf_op jit(solution)/shard_map/while/body/eval_jaxpr/hij,hjk->hik/dot_general | solution.py:104
  565.9 6.1 %fusion.107 = f32[8,128,256]{1,2,0:T(8,128)} fusion(f32[8,128,256]{1,2,0:T(8,128)S(1)} %copy.216, f32[4,8,256,256]{3,2,1,0:T(8,128)} %get-tuple-element.406, s32[]{:T(128)} %get-tuple-element.397, f32[1,8,128,256]{2,3,1,0:T(8,128)S(1)} %copy-done, pred[]{:T(512)S(6)} %lt.43), kind=kOutput, calls=%fused_computation.5.clone.1 | convolution fusion | flops 805830656 | bytes 6291969 | tf_op jit(solution)/shard_map/while/body/eval_jaxpr/hij,hjk->hik/dot_general | solution.py:104
  576.2 6.1 %fusion.107 = f32[8,128,256]{1,2,0:T(8,128)} fusion(f32[8,128,256]{1,2,0:T(8,128)S(1)} %copy.216, f32[4,8,256,256]{3,2,1,0:T(8,128)} %get-tuple-element.406, s32[]{:T(128)} %get-tuple-element.397, f32[1,8,128,256]{2,3,1,0:T(8,128)S(1)} %copy-done, pred[]{:T(512)S(6)} %lt.43), kind=kOutput, calls=%fused_computation.5.clone.1 | convolution fusion | flops 805830656 | bytes 6291969 | tf_op jit(solution)/shard_map/while/body/eval_jaxpr/hij,hjk->hik/dot_general | solution.py:104
  582.3 4.0 convolution_add_fusion
  589.4 2.5 fusion.45
  (157 shorter events, 57.5 us)
Async XLA Ops:
  6.5 108.9 %all-gather.13.cloned.1.call-start = ((), (), s32[]{:S(2)}) async-start(), calls=%async_computation.3 | async-start | bytes 5242880 | tf_op jit(solution)/shard_map/all_gather | solution.py:9
  6.6 6.9 %copy-start.25 = (pred[256,256]{1,0:T(8,128)(4,1)}, pred[256,256]{1,0:T(8,128)(4,1)S(1)}, u32[]{:S(2)}) copy-start(pred[256,256]{1,0:T(8,128)(4,1)S(1)} %iota_compare_fusion) | copy-start | bytes 196612
  8.2 5.3 copy-start.28
  10.5 3.0 copy-start.31
  10.5 3.0 copy-start.27
  10.5 4.4 copy-start.21
  18.3 2.1 copy-start.23
  20.4 16.1 %copy-start.2 = (f32[256,8,128]{2,1,0:T(8,128)}, f32[256,8,128]{2,1,0:T(8,128)S(1)}, u32[]{:S(2)}) copy-start(f32[256,8,128]{2,1,0:T(8,128)S(1)} %get-tuple-element.291) | copy-start | bytes 3145732
  24.8 1.7 copy-start.6
  29.2 3.0 copy-start.32
  29.2 3.0 copy-start.26
  29.2 3.0 copy-start.29
  29.2 3.0 copy-start.30
  31.8 233.4 %all-gather.11.cloned.1.call-start = ((), (), s32[]{:S(2)}) async-start(), calls=%async_computation.2 | async-start | bytes 10485760 | tf_op jit(solution)/shard_map/all_gather | solution.py:9
  35.1 2.9 copy-start.8
  35.1 2.9 copy-start.10
  40.7 404.2 %all-reduce.3.cloned.1.call-start = ((), (), s32[]{:S(2)}) async-start(), calls=%async_computation.4 | async-start | bytes 6291456 | tf_op jit(solution)/shard_map/psum | solution.py:23
  315.1 5.2 copy-start.9
  315.1 5.2 copy-start.11
  315.1 5.2 copy-start.13
  315.1 5.2 copy-start.15
  325.2 156.0 %all-gather.9.cloned.1.call-start = ((), (), s32[]{:S(2)}) async-start(), calls=%async_computation.1 | async-start | bytes 5242880 | tf_op jit(solution)/shard_map/all_gather | solution.py:138
  447.5 2.0 copy-start.24
  447.5 93.4 %all-gather.7.cloned.1.call-start = ((), (), s32[]{:S(2)}) async-start(), calls=%async_computation | async-start | bytes 10485760 | tf_op jit(solution)/shard_map/all_gather | solution.py:137
  452.1 5.1 copy-start.1
  543.8 1.5 copy-start
  554.1 1.5 copy-start
  564.4 1.5 copy-start
  574.7 1.5 copy-start
  582.3 4.0 copy-start.4
  586.3 2.5 copy-start.17
  587.6 1.7 copy-start.5
  (9 other events, 9.9 us)
Sparse Core Ops, SparseCore 0:
  31.9 83.4 all-gather.12
  117.0 148.1 all-gather.10
  325.3 119.6 all-reduce.2
  447.7 33.4 all-gather.8
  482.6 58.2 all-gather.6
where the time goes:
time: 609 us; the launch traced here: 601 us
  waiting for transfers between devices  427 us (70%)
  matrix products  93.8 us (15%)
  local copies, waits for them, and re-layouts  56.5 us (9%)
  between operations  13.9 us (2%)
  other arithmetic  8.6 us (1%)
    all_gather x2, waiting for transfers between devices, carried_in(): pieces = jax.tree.map(lambda part: lax.all_gather(part, axis), value)  224 us
    psum x1, waiting for transfers between devices, from_root(): return lax.psum(block, axis)  120 us
    all_gather x1, waiting for transfers between devices, local(): lax.all_gather(group_map[0][None], 'outer', axis=0, tiled=True)  59.7 us
    dot_general x9, matrix products, advance_state(): jnp.einsum('hij,hjk->hik', carried, transition, precision=lax.Precision.H...  51.8 us
    all_gather x1, waiting for transfers between devices, local(): lax.all_gather(group_map[1][None], 'outer', axis=0, tiled=True)  22.6 us
    dot_general x4, matrix products, compose(): jnp.einsum('hij,hjk->hik', earlier[0], later[0], precision=lax.Precision....  20.2 us
  transfers between devices with their start and end apart: 5, of which 5 were waited for; matrix products, arithmetic and copies ran while one was open for 3% of the time, Pallas kernels for 0%

commit v1 on v0

--- a/solution.py
+++ b/solution.py
@@ -120,6 +120,20 @@
 
 
 def local(queries, keys, values, retain, step, momentum, init_memory, init_momentum):
+
+    def play_the_turns(local_array):
+        mesh_name = "outer"
+        world_n = lax.axis_size(mesh_name)
+        tray = [local_array]
+        for tick in range(1, world_n):
+            clean = lax.ppermute(
+                tray[tick - 1], mesh_name, [(ii, (ii - 1) % world_n) for ii in range(world_n)]
+            )
+            tray.append(clean)
+        carry_in = jnp.concatenate(tray, 0)
+        ready = jnp.roll(carry_in, lax.axis_index(mesh_name) * local_array.shape[0], axis=0)
+        return ready
+
     transition, offset, local_terms = block_terms(queries, keys, values, retain, step, momentum)
     identity_maps = (
         jnp.broadcast_to(jnp.eye(transition.shape[1], dtype=jnp.float32), transition.shape),
@@ -135,7 +149,7 @@
     )
     gathered = (
         lax.all_gather(group_map[0][None], "outer", axis=0, tiled=True),
-        lax.all_gather(group_map[1][None], "outer", axis=0, tiled=True),
+        play_the_turns(group_map[1][None]),
     )
     entry_state = apply_earlier(gathered, first_state)
     block_state = advance_state(entry_state, before[0], before[1])

time: 609 us -> 580 us (0.952)
  waiting for transfers between devices: 427 us -> 402 us
  local copies, waits for them, and re-layouts: 56.5 us -> 50.4 us
    all_gather x1, waiting for transfers between devices: 59.7 us -> 0.01 us  [local(): lax.all_gather(group_map[0][None], 'outer', axis=0, tiled=True)]
    ppermute x0 -> x3, waiting for transfers between devices: none -> 58.8 us  [play_the_turns(): lax.ppermute(tray[tick - 1], mesh_name, [(ii, (ii - 1) % world_n) for ii...]
    all_gather x1 -> x0, waiting for transfers between devices: 22.6 us -> none  [local(): lax.all_gather(group_map[1][None], 'outer', axis=0, tiled=True)]
    unnamed x69 -> x80, local copies, waits for them, and re-layouts: 7.74 us -> 16.5 us
    dynamic_slice x8 -> x1, local copies, waits for them, and re-layouts: 10.7 us -> 2.31 us  [play_the_turns(): jnp.roll(carry_in, lax.axis_index(mesh_name) * local_array.shape[0], axis=0)]
  transfers between devices with their start and end apart: 5 -> 7, of which waited for: 5 -> 6; matrix products, arithmetic and copies ran while one was open for 3% -> 5% of each run, Pallas kernels for 0% -> 0%
where the time goes in v1:
time: 580 us; the launch traced here: 573 us
  waiting for transfers between devices  402 us (69%)
  matrix products  90.7 us (16%)
  local copies, waits for them, and re-layouts  50.4 us (9%)
  between operations  14 us (2%)
  other arithmetic  8.09 us (1%)
  starting transfers between devices  6.37 us (1%)
    all_gather x2, waiting for transfers between devices, carried_in(): pieces = jax.tree.map(lambda part: lax.all_gather(part, axis), value)  224 us
    psum x1, waiting for transfers between devices, from_root(): return lax.psum(block, axis)  120 us
    ppermute x3, waiting for transfers between devices, play_the_turns(): lax.ppermute(tray[tick - 1], mesh_name, [(ii, (ii - 1) % world_n) for ii...  58.8 us
    dot_general x9, matrix products, advance_state(): jnp.einsum('hij,hjk->hik', carried, transition, precision=lax.Precision.H...  48.9 us
    dot_general x4, matrix products, compose(): jnp.einsum('hij,hjk->hik', earlier[0], later[0], precision=lax.Precision....  20.2 us
    unnamed x80, local copies, waits for them, and re-layouts  16.5 us
    dynamic_slice x6, local copies, waits for them, and re-layouts, turn(): longer = join(total, jax.tree.map(lambda part: part[position], pieces))  11.6 us
  transfers between devices with their start and end apart: 7, of which 6 were waited for; matrix products, arithmetic and copies ran while one was open for 5% of the time, Pallas kernels for 0%

profile of v1, /device:TPU:0, one launch (start us, length us, event | category | flops | bytes accessed | tf_op | source)
XLA Modules:
  0.0 572.6 jit_solution(14065272494016560587)
XLA Ops:
  10.5 2.9 fusion.39
  28.6 2.6 copy.125
  31.6 2.3 fusion.44
  40.9 74.0 %all-gather.10.cloned.1.call-done = f32[32,128,256]{2,1,0:T(8,128)} async-done(((f32[8,128,256]{2,1,0:T(8,128)}), f32[32,128,256]{2,1,0:T(8,128)}) %all-gather.10.cloned.1.call-update) | async-done | bytes 4194320 | tf_op jit(solution)/shard_map/all_gather | solution.py:9
  114.9 149.8 %all-gather.8.cloned.1.call-done = f32[32,256,256]{2,1,0:T(8,128)} async-done(((f32[8,256,256]{2,1,0:T(8,128)}), f32[32,256,256]{2,1,0:T(8,128)}) %all-gather.8.cloned.1.call-update) | async-done | bytes 8388624 | tf_op jit(solution)/shard_map/all_gather | solution.py:9
  264.8 49.7 %while.30 = (s32[]{:T(128)}, f32[8,256,256]{1,2,0:T(8,128)S(1)}, f32[8,128,256]{1,2,0:T(8,128)}, s32[]{:T(128)}, f32[4,8,256,256]{3,2,1,0:T(8,128)}, /*index=5*/f32[4,8,128,256]{3,2,1,0:T(8,128)}, s32[]{:T(128)}, s32[]{:T(128)}) while((s32[]{:T(128)}, f32[8,256,256]{1,2,0:T(8,128)S(1)}, f32[8,128,256]{1,2,0:T(8,128)}, s32[]{:T(128)}, ...), condition=%wide.region_7.8_spmd.clone, body=%wide.region_6.7_spmd.clone.sunk | while | flops 2417491968 | bytes 25168492 | solution.py:18
  264.8 2.3 constant_dynamic-slice_fusion.3
  269.9 6.1 %fusion.112 = f32[8,128,256]{1,2,0:T(8,128)} fusion(f32[4,8,256,256]{3,2,1,0:T(8,128)} %get-tuple-element.387, s32[]{:T(128)} %get-tuple-element.375, f32[1,8,128,256]{2,3,1,0:T(8,128)S(1)} %copy.188, f32[8,128,256]{1,2,0:T(8,128)S(1)} %copy.220, pred[]{:T(512)S(6)} %compare.4, pred[]{:T(512)S(6)} %lt.58), kind=kOutput, calls=%fused_computation.16.clone.1 | convolution fusion | flops 806354944 | bytes 6293504 | tf_op jit(solution)/shard_map/while/body/eval_jaxpr/hij,hjk->hik/dot_general | solution.py:104
  276.2 5.1 bitcast_select_fusion.2
  281.4 2.3 constant_dynamic-slice_fusion.3
  286.5 6.1 %fusion.112 = f32[8,128,256]{1,2,0:T(8,128)} fusion(f32[4,8,256,256]{3,2,1,0:T(8,128)} %get-tuple-element.387, s32[]{:T(128)} %get-tuple-element.375, f32[1,8,128,256]{2,3,1,0:T(8,128)S(1)} %copy.188, f32[8,128,256]{1,2,0:T(8,128)S(1)} %copy.220, pred[]{:T(512)S(6)} %compare.4, pred[]{:T(512)S(6)} %lt.58), kind=kOutput, calls=%fused_computation.16.clone.1 | convolution fusion | flops 806354944 | bytes 6293504 | tf_op jit(solution)/shard_map/while/body/eval_jaxpr/hij,hjk->hik/dot_general | solution.py:104
  292.7 5.1 bitcast_select_fusion.2
  297.9 2.3 constant_dynamic-slice_fusion.3
  303.0 6.1 %fusion.112 = f32[8,128,256]{1,2,0:T(8,128)} fusion(f32[4,8,256,256]{3,2,1,0:T(8,128)} %get-tuple-element.387, s32[]{:T(128)} %get-tuple-element.375, f32[1,8,128,256]{2,3,1,0:T(8,128)S(1)} %copy.188, f32[8,128,256]{1,2,0:T(8,128)S(1)} %copy.220, pred[]{:T(512)S(6)} %compare.4, pred[]{:T(512)S(6)} %lt.58), kind=kOutput, calls=%fused_computation.16.clone.1 | convolution fusion | flops 806354944 | bytes 6293504 | tf_op jit(solution)/shard_map/while/body/eval_jaxpr/hij,hjk->hik/dot_general | solution.py:104
  309.2 5.1 bitcast_select_fusion.2
  314.6 5.3 fusion.49
  319.9 4.8 select_bitcast_fusion
  324.8 119.7 %all-reduce.3.cloned.1.call-done = (f32[1,8,256,256]{3,2,1,0:T(8,128)}, f32[1,8,128,256]{2,3,1,0:T(8,128)}) async-done(((f32[1,8,256,256]{3,2,1,0:T(8,128)}, f32[1,8,128,256]{2,3,1,0:T(8,128)}), (f32[1,8,256,256]{3,2,1,0:T(8,128)}, f32[1,8,128,256]{2,3,1,0:T(8,128)})) %all-reduce.3.cloned.1.call-update) | async-done | bytes 3145744 | tf_op jit(solution)/shard_map/psum | solution.py:23
  445.5 19.7 %collective-permute-done = f32[1,8,128,256]{2,3,1,0:T(8,128)S(1)} collective-permute-done((f32[1,8,128,256]{2,3,1,0:T(8,128)}, f32[1,8,128,256]{2,3,1,0:T(8,128)S(1)}, u32[]{:S(2)}, u32[]{:S(2)}) %collective-permute-start) | collective-permute-done | bytes 1048608 | tf_op jit(solution)/shard_map/ppermute | solution.py:129
  468.4 34.8 %collective-permute-done.1 = f32[1,8,128,256]{2,3,1,0:T(8,128)} collective-permute-done((f32[1,8,128,256]{2,3,1,0:T(8,128)S(1)}, f32[1,8,128,256]{2,3,1,0:T(8,128)}, u32[]{:S(2)}, u32[]{:S(2)}) %collective-permute-start.1) | collective-permute-done | bytes 1048608 | tf_op jit(solution)/shard_map/ppermute | solution.py:129
  503.2 2.3 collective-permute-start.2
  510.8 4.9 fusion.66
  515.7 2.5 copy.136
  521.2 4.3 collective-permute-done.2
  529.6 2.3 constant_dynamic-slice_fusion.1
  531.9 22.2 %while.29 = (s32[]{:T(128)}, f32[8,128,256]{1,2,0:T(8,128)S(1)}, s32[]{:T(128)}, f32[4,8,256,256]{3,2,1,0:T(8,128)}, f32[4,8,128,256]{2,3,1,0:T(8,128)}, /*index=5*/s32[]{:T(128)}) while((s32[]{:T(128)}, f32[8,128,256]{1,2,0:T(8,128)S(1)}, s32[]{:T(128)}, f32[4,8,256,256]{3,2,1,0:T(8,128)}, f32[4,8,128,256]{2,3,1,0:T(8,128)}, ...), condition=%wide.region_11.12_spmd, body=%wide.region_10.11_spmd.sunk | while | flops 805830656 | bytes 8389711 | solution.py:119
  532.2 5.4 fusion.107
  537.7 5.4 fusion.107
  543.2 5.4 fusion.107
  548.7 5.4 fusion.107
  554.2 3.7 convolution_add_fusion
  560.9 2.6 fusion.45
  (156 shorter events, 57.1 us)
Async XLA Ops:
  6.5 108.3 %all-gather.10.cloned.1.call-start = ((), (), s32[]{:S(2)}) async-start(), calls=%async_computation.2 | async-start | bytes 5242880 | tf_op jit(solution)/shard_map/all_gather | solution.py:9
  6.6 6.9 %copy-start.26 = (pred[256,256]{1,0:T(8,128)(4,1)}, pred[256,256]{1,0:T(8,128)(4,1)S(1)}, u32[]{:S(2)}) copy-start(pred[256,256]{1,0:T(8,128)(4,1)S(1)} %iota_compare_fusion) | copy-start | bytes 196612
  8.2 5.3 copy-start.29
  10.5 4.3 copy-start.32
  10.5 4.3 copy-start.28
  10.5 4.5 copy-start.22
  17.7 2.1 copy-start.24
  19.9 16.1 %copy-start = (f32[256,8,128]{2,1,0:T(8,128)}, f32[256,8,128]{2,1,0:T(8,128)S(1)}, u32[]{:S(2)}) copy-start(f32[256,8,128]{2,1,0:T(8,128)S(1)} %get-tuple-element.291) | copy-start | bytes 3145732
  24.2 1.7 copy-start.4
  28.6 3.0 copy-start.33
  28.6 3.0 copy-start.27
  28.6 3.0 copy-start.30
  28.6 3.0 copy-start.31
  31.2 233.4 %all-gather.8.cloned.1.call-start = ((), (), s32[]{:S(2)}) async-start(), calls=%async_computation.1 | async-start | bytes 10485760 | tf_op jit(solution)/shard_map/all_gather | solution.py:9
  34.5 2.9 copy-start.6
  34.5 2.9 copy-start.8
  40.2 404.3 %all-reduce.3.cloned.1.call-start = ((), (), s32[]{:S(2)}) async-start(), calls=%async_computation.3 | async-start | bytes 6291456 | tf_op jit(solution)/shard_map/psum | solution.py:23
  314.6 5.3 copy-start.7
  314.6 5.3 copy-start.9
  314.6 5.3 copy-start.11
  314.6 5.3 copy-start.13
  324.7 180.8 %copy-start.5 = (bf16[256,1024]{0,1:T(8,128)(2,1)S(1)}, bf16[256,1024]{0,1:T(8,128)(2,1)}, u32[]{:S(2)}) copy-start(bf16[256,1024]{0,1:T(8,128)(2,1)} %copy.120) | copy-start | bytes 1572868
  324.7 181.7 %copy-start.25 = (f32[8,128,128]{2,1,0:T(8,128)S(1)}, f32[8,128,128]{2,1,0:T(8,128)}, u32[]{:S(2)}) copy-start(f32[8,128,128]{2,1,0:T(8,128)} %param.18) | copy-start | bytes 1572868
  324.7 207.2 %all-gather.6.cloned.1.call-start = ((), (), s32[]{:S(2)}) async-start(), calls=%async_computation | async-start | bytes 10485760 | tf_op jit(solution)/shard_map/all_gather | solution.py:151
  444.6 20.7 %collective-permute-start = (f32[1,8,128,256]{2,3,1,0:T(8,128)}, f32[1,8,128,256]{2,3,1,0:T(8,128)S(1)}, u32[]{:S(2)}, u32[]{:S(2)}) collective-permute-start(f32[1,8,128,256]{2,3,1,0:T(8,128)} %get-tuple-element.287), channel_id=1, source_target_pairs={{0,3},{1,0},{2,1},{3,2},{4,7},{5,4},{6,5},{7,6},{8,11},{9,8},{10,9... | collective-permute-start | bytes 3145736 | tf_op jit(solution)/shard_map/ppermute | solution.py:129
  466.2 37.0 %collective-permute-start.1 = (f32[1,8,128,256]{2,3,1,0:T(8,128)S(1)}, f32[1,8,128,256]{2,3,1,0:T(8,128)}, u32[]{:S(2)}, u32[]{:S(2)}) collective-permute-start(f32[1,8,128,256]{2,3,1,0:T(8,128)S(1)} %collective-permute-done), channel_id=1, source_target_pairs={{0,3},{1,0},{2,1},{3,2},{4,7},{5,4},{6,5},{7,6},{8,11},{9,8},{10,9... | collective-permute-start | bytes 3145736 | tf_op jit(solution)/shard_map/ppermute | solution.py:129
  503.2 22.4 %collective-permute-start.2 = (f32[1,8,128,256]{2,3,1,0:T(8,128)}, f32[1,8,128,256]{2,3,1,0:T(8,128)}, u32[]{:S(2)}, u32[]{:S(2)}) collective-permute-start(f32[1,8,128,256]{2,3,1,0:T(8,128)} %collective-permute-done.1), channel_id=1, source_target_pairs={{0,3},{1,0},{2,1},{3,2},{4,7},{5,4},{6,5},{7,6},{8,11},{9,8},{10,9... | collective-permute-start | bytes 3145736 | tf_op jit(solution)/shard_map/ppermute | solution.py:129
  518.2 1.5 copy-start.16
  519.8 7.0 %copy-start.14 = (f32[1,8,128,256]{2,3,1,0:T(8,128)S(1)}, f32[1,8,128,256]{2,3,1,0:T(8,128)}, u32[]{:S(2)}) copy-start(f32[1,8,128,256]{2,3,1,0:T(8,128)} %get-tuple-element.287) | copy-start | bytes 3145732
  554.1 3.7 copy-start.2
  557.9 2.5 copy-start.18
  559.2 1.7 copy-start.3
  (9 other events, 9.9 us)
Sparse Core Ops, SparseCore 0:
  31.4 83.4 all-gather.9
  116.4 148.1 all-gather.7
  324.9 119.6 all-reduce.2
  446.0 75.8 all-gather.5
